TPU v7x, 32 devices: a whole 2x2x4 slice. The times are simulated.
32 devices in a mesh: sta: 4 (over y, x), evt: 8 (over z, core).
Axes of the slice: x: 2, y: 2, z: 4, core: 2. Of those that a mesh axis runs over, the one named last changes fastest.
Arguments:
- traces: bfloat16 [3, 32, 512, 2048], P(None, 'sta', 'evt'), may hold values from -96 to 96
- baz_bin: int32 [32, 512], P('sta', 'evt'), may hold values from 0 to 35
- inc_bin: int32 [32, 512], P('sta', 'evt'), may hold values from 0 to 7
- counts: int32 [32], P('sta'), may hold values from 64 to 512
- depth_index: int32 [32, 512], P('sta'), may hold values from 0 to 2046
- tile_of: int32 [32], replicated, may hold values from 0 to 15
Outputs:
- stack: float32 [16, 5, 2, 512], P('sta', None, None, 'evt')
All inputs are finite; a program needn't handle non-finite values.
Results may differ from a plain program's by a relative error of at most 0.0003.
Values sent between devices are 32-bit elements; how exact they have to be, the bound alone decides.
A program may use at most 64 MiB of HBM per device.

v0:
```python
import jax
import jax.numpy as jnp
from jax import lax
from jax.sharding import PartitionSpec as P

NS = 2048
DEPTHS = 512
BAZ_BINS = 36
TILE_DEV = 4


def solve_blocks(normal, right):
    factor = jnp.linalg.cholesky(normal)
    middle = jax.scipy.linalg.solve_triangular(factor, right, lower=True)
    return jax.scipy.linalg.solve_triangular(factor, middle, lower=True, trans=1)


def to_depths(values, indices):
    picks = indices[:, None, None, :]
    first = jnp.take_along_axis(values, picks, axis=3)
    second = jnp.take_along_axis(values, picks + 1, axis=3)
    return 0.5 * (first + second)


def body(traces, baz_bin, inc_bin, counts, depth_index, tile_of):
    highest = lax.Precision.HIGHEST
    stations = traces.shape[1]
    slots = traces.shape[2]
    evt_count = lax.axis_size("evt")
    depth_share = DEPTHS // evt_count
    phi = (baz_bin.astype(jnp.float32) + 0.5) * (2.0 * jnp.pi / BAZ_BINS)
    incidence = (12.0 + 2.5 * (inc_bin.astype(jnp.float32) + 0.5)) * (jnp.pi / 180.0)
    cosine = jnp.cos(phi)[:, :, None]
    sine = jnp.sin(phi)[:, :, None]
    vertical = traces[0].astype(jnp.float32)
    north = traces[1].astype(jnp.float32)
    east = traces[2].astype(jnp.float32)
    radial = -(cosine * north + sine * east)
    quality = jnp.cos(incidence)[:, :, None] * radial + jnp.sin(incidence)[:, :, None] * vertical
    transverse = sine * north - cosine * east
    data = jnp.concatenate([quality, transverse], axis=2)
    slot_ids = lax.axis_index("evt") * slots + jnp.arange(slots)
    live = (slot_ids[None, :] < counts[:, None]).astype(jnp.float32)
    harm = jnp.stack(
        [jnp.ones_like(phi), jnp.cos(phi), jnp.sin(phi), jnp.cos(2.0 * phi), jnp.sin(2.0 * phi)],
        axis=2,
    )
    weighted = harm * live[:, :, None]
    normal_part = jnp.einsum("sek,sel->skl", weighted, harm, precision=highest)
    rhs_part = jnp.einsum("sek,sec->skc", weighted, data, precision=highest)
    normal = lax.psum(normal_part, "evt") + jnp.eye(5, dtype=jnp.float32)[None]
    shares = lax.psum_scatter(rhs_part, "evt", scatter_dimension=2, tiled=True)
    solved = solve_blocks(normal, shares)
    coeff = lax.all_gather(solved, "evt", axis=2, tiled=True).reshape(stations, 5, 2, NS)
    mine = lax.dynamic_slice_in_dim(
        depth_index, lax.axis_index("evt") * depth_share, depth_share, 1
    )
    profile = to_depths(coeff, mine)
    first_tile = lax.axis_index("sta") * TILE_DEV
    own_tiles = first_tile + jnp.arange(TILE_DEV)
    members = jnp.sum((tile_of[None, :] == own_tiles[:, None]).astype(jnp.float32), axis=1)
    everyone = lax.all_gather(profile, "sta", axis=0, tiled=True)
    onehot = (tile_of[None, :] == own_tiles[:, None]).astype(jnp.float32)
    sums = jnp.einsum("ts,skcz->tkcz", onehot, everyone, precision=highest)
    return sums / jnp.maximum(members, 1.0)[:, None, None, None]


def solution(mesh):
    return jax.shard_map(
        body,
        mesh=mesh,
        in_specs=(
            P(None, "sta", "evt", None),
            P("sta", "evt"),
            P("sta", "evt"),
            P("sta"),
            P("sta", None),
            P(),
        ),
        out_specs=P("sta", None, None, "evt"),
        check_vma=False,
    )
```

profile of v0, /device:TPU:0, one launch (start us, length us, event | category | flops | bytes accessed | tf_op | source)
XLA Modules:
  0.0 130.2 jit_solution(14801742810654873437)
XLA Ops:
  6.5 0.8 fusion.24
  7.3 0.7 compare_convert_fusion
  8.0 6.8 %fusion.7 = (f32[8,64,2048]{2,1,0:T(8,128)}, f32[8,64,2048]{2,1,0:T(8,128)}) fusion(bf16[3,8,64,2048]{3,2,1,0:T(8,128)(2,1)} %param.8, f32[8,64]{1,0:T(8,128)S(1)} %get-tuple-element.18, f32[8,64]{1,0:T(8,128)S(1)} %get-tuple-element.13, f32[8,64]{1,0:T(8,128)S(1)} %get-tuple-element.15, f32[8,64]{1,0:T(8,128)S(1)} %get-tuple-element.19), kind=kLoop, calls=%fused_computation.13 | loop fusion | flops 13631488 | bytes 14688256 | tf_op jit(solution)/shard_map/add | solution.py:39
  14.9 7.3 %fusion = f32[8,5,4096]{2,1,0:T(8,128)} fusion(f32[8,64,2048]{2,1,0:T(8,128)} %get-tuple-element.7, f32[8,64,2048]{2,1,0:T(8,128)} %get-tuple-element.6, f32[8,64,5]{1,2,0:T(8,128)S(1)} %stack.19, f32[8,64]{1,0:T(8,128)S(1)} %compare_convert_fusion), kind=kOutput, calls=%fused_computation.2 | convolution fusion | flops 127928832 | bytes 9056256 | tf_op jit(solution)/shard_map/sek,sec->skc/dot_general | solution.py:50
  22.2 0.2 fusion.10
  22.4 30.3 %psum.7 = f32[8,5,5]{1,2,0:T(8,128)S(1)} all-reduce(f32[8,5,5]{1,2,0:T(8,128)S(1)} %fusion.10), channel_id=1, replica_groups=mesh['sta'=4,'evt'=8] {'evt'}, use_global_device_ids=true, to_apply=%region_0.0 | all-reduce | flops 200 | bytes 1600 | tf_op jit(solution)/shard_map/psum | solution.py:51
  52.9 0.1 copy.31
  53.0 3.7 %custom-call.11 = f32[8,5,5]{2,1,0:T(8,128)S(1)} custom-call(f32[8,5,5]{2,1,0:T(8,128)S(1)} %fusion.17), custom_call_target="Cholesky" | custom-call | tf_op jit(solution)/shard_map/jit(cholesky)/cholesky | solution.py:13
  56.7 0.1 compare_reduce_fusion
  56.9 3.2 %custom-call.12 = f32[8,1,5,5]{2,3,1,0:T(8,128)S(1)} custom-call(f32[8,1,5,5]{3,2,1,0:T(8,128)S(1)} %select_bitcast_fusion), custom_call_target="InvertDiagBlocksLowerTriangular" | custom-call | tf_op jit(solution)/shard_map/jit(_solve_triangular)/vmap()/triangular_solve | solution.py:15
  60.1 0.1 bitcast_or_fusion.1
  60.5 0.2 fusion.28
  60.7 1.2 fusion.15
  61.9 0.3 fusion.13
  62.2 16.4 %all_gather.6 = f32[8,5,4096]{2,1,0:T(8,128)S(1)} all-gather(f32[8,5,512]{2,1,0:T(8,128)S(1)} %fusion.13), channel_id=1, replica_groups=mesh['sta'=4,'evt'=8] {'evt'}, dimensions={2}, use_global_device_ids=true | all-gather | bytes 737280 | tf_op jit(solution)/shard_map/all_gather | solution.py:54
  78.5 0.6 reshape.133
  79.1 17.0 %copy.34 = f32[8,5,2,2048]{1,2,3,0:T(2,128)} copy(f32[8,5,2,2048]{3,2,1,0:T(2,128)S(1)} %reshape.133) | data formatting | bytes 1310720 | tf_op jit(solution)/shard_map/reshape | solution.py:54
  96.1 8.3 %gather_fusion = f32[512,5,2]{1,2,0:T(2,128)S(1)} fusion(f32[8,5,2,2048]{1,2,3,0:T(2,128)} %copy.34, s32[512]{0:T(512)S(1)} %reshape.123), kind=kCustom, calls=%fused_computation.clone | custom fusion | bytes 45056 | tf_op jit(solution)/shard_map/jit(take_along_axis)/gather | solution.py:20
  104.4 0.2 copy.44
  104.6 8.3 %gather_fusion.1 = f32[512,5,2]{1,2,0:T(2,128)S(1)} fusion(f32[8,5,2,2048]{1,2,3,0:T(2,128)} %copy.34, s32[512]{0:T(512)S(1)} %reshape.128), kind=kCustom, calls=%fused_computation.1.clone | custom fusion | bytes 45056 | tf_op jit(solution)/shard_map/jit(take_along_axis)/gather | solution.py:21
  113.0 0.2 copy.46
  113.2 9.3 %all_gather.7 = f32[32,5,2,64]{3,0,2,1:T(8,128)S(1)} all-gather(f32[8,5,2,64]{3,0,2,1:T(8,128)S(1)} %fusion.12), channel_id=1, replica_groups=mesh['sta'=4,'evt'=8] {'sta'}, dimensions={0}, use_global_device_ids=true | all-gather | bytes 102400 | tf_op jit(solution)/shard_map/all_gather | solution.py:62
  122.6 0.2 convolution_divide_fusion
  122.8 0.6 copy.38
  (24 shorter events, 0.6 us)
Async XLA Ops:
  6.5 54.2 %reduce-scatter.2.cloned.1.call-start = ((), (), s32[]{:S(2)}) async-start(), calls=%async_computation.1 | async-start | bytes 1179648 | tf_op jit(solution)/shard_map/reduce_scatter | solution.py:52
  14.9 45.2 %copy-start = (s32[8,512]{1,0:T(8,128)S(1)}, s32[8,512]{1,0:T(8,128)}, u32[]{:S(2)}) copy-start(s32[8,512]{1,0:T(8,128)} %param.12) | copy-start | bytes 49156
  14.9 45.6 %copy-start.1 = (s32[32]{0:T(128)S(1)}, s32[32]{0:T(128)}, u32[]{:S(2)}) copy-start(s32[32]{0:T(128)} %param.13) | copy-start | bytes 388
Sparse Core Ops, SparseCore 0:
  22.3 35.4 reduce-scatter.1
where the time goes:
time: 131 us; the launch traced here: 130 us
  blocking collectives  56 us (43%)
  local copies, waits for them, and re-layouts  35.7 us (27%)
  other arithmetic  15.8 us (12%)
  between operations  13.5 us (10%)
  matrix products  9.13 us (7%)
    psum x1, blocking collectives, body(): normal = lax.psum(normal_part, 'evt') + jnp.eye(5, dtype=jnp.float32)[None]  30.3 us
    reshape x2, local copies, waits for them, and re-layouts, body(): lax.all_gather(solved, 'evt', axis=2, tiled=True)  17.5 us
    all_gather x1, blocking collectives, body(): lax.all_gather(solved, 'evt', axis=2, tiled=True)  16.4 us
    all_gather x1, blocking collectives, body(): everyone = lax.all_gather(profile, 'sta', axis=0, tiled=True)  9.34 us
    gather x3, local copies, waits for them, and re-layouts, to_depths(): second = jnp.take_along_axis(values, picks + 1, axis=3)  8.62 us
    gather x3, local copies, waits for them, and re-layouts, to_depths(): first = jnp.take_along_axis(values, picks, axis=3)  8.62 us
    dot_general x1, matrix products, body(): rhs_part = jnp.einsum('sek,sec->skc', weighted, data, precision=highest)  7.27 us
    add x1, other arithmetic, body(): jnp.cos(incidence)[:, :, None] * radial  6.81 us
  transfers between devices with their start and end apart: 1, of which 0 were waited for; matrix products, arithmetic and copies ran while one was open for 6% of the time, Pallas kernels for 0%

commit v1 on v0

--- a/solution.py
+++ b/solution.py
@@ -7,6 +7,18 @@
 DEPTHS = 512
 BAZ_BINS = 36
 TILE_DEV = 4
+
+
+def product_in_turn(x, axis, dim, term):
+    count, index, rows = (lax.axis_size(axis), lax.axis_index(axis), x.shape[dim])
+    right = [(i, (i + 1) % count) for i in range(count)]
+    current, subtotal = (x, None)
+    for hop in range(count):
+        coming = lax.ppermute(current, axis, right) if hop < count - 1 else None
+        update = term(current, (index - hop) % count * rows)
+        subtotal = update if subtotal is None else subtotal + update
+        current = coming
+    return subtotal
 
 
 def solve_blocks(normal, right):
@@ -59,9 +71,18 @@
     first_tile = lax.axis_index("sta") * TILE_DEV
     own_tiles = first_tile + jnp.arange(TILE_DEV)
     members = jnp.sum((tile_of[None, :] == own_tiles[:, None]).astype(jnp.float32), axis=1)
-    everyone = lax.all_gather(profile, "sta", axis=0, tiled=True)
     onehot = (tile_of[None, :] == own_tiles[:, None]).astype(jnp.float32)
-    sums = jnp.einsum("ts,skcz->tkcz", onehot, everyone, precision=highest)
+    sums = product_in_turn(
+        profile,
+        "sta",
+        0,
+        lambda part, at: jnp.einsum(
+            "ts,skcz->tkcz",
+            lax.dynamic_slice_in_dim(onehot, at, part.shape[0], axis=1),
+            part,
+            precision=highest,
+        ),
+    )
     return sums / jnp.maximum(members, 1.0)[:, None, None, None]
 
 

time: 131 us -> 136 us (1.038)
  waiting for transfers between devices: 0.04 us -> 12 us
  blocking collectives: 56 us -> 47 us
  starting transfers between devices: 0.01 us -> 2.13 us
    ppermute x0 -> x3, waiting for transfers between devices: none -> 12 us  [product_in_turn(): coming = lax.ppermute(current, axis, right) if hop < count - 1 else None]
    all_gather x1 -> x0, blocking collectives: 9.34 us -> none  [body(): everyone = lax.all_gather(profile, 'sta', axis=0, tiled=True)]
    ppermute x0 -> x3, starting transfers between devices: none -> 2.12 us  [product_in_turn(): coming = lax.ppermute(current, axis, right) if hop < count - 1 else None]
  transfers between devices with their start and end apart: 1 -> 4, of which waited for: 0 -> 3; matrix products, arithmetic and copies ran while one was open for 6% -> 6% of each run, Pallas kernels for 0% -> 0%
where the time goes in v1:
time: 136 us
  blocking collectives  47 us (35%)
  local copies, waits for them, and re-layouts  35.7 us (26%)
  other arithmetic  15.8 us (12%)
  between operations  13.6 us (10%)
  waiting for transfers between devices  12 us (9%)
  matrix products  9.76 us (7%)
  starting transfers between devices  2.13 us (2%)
    psum x1, blocking collectives, body(): normal = lax.psum(normal_part, 'evt') + jnp.eye(5, dtype=jnp.float32)[None]  30.6 us
    reshape x2, local copies, waits for them, and re-layouts, body(): lax.all_gather(solved, 'evt', axis=2, tiled=True)  17.5 us
    all_gather x1, blocking collectives, body(): lax.all_gather(solved, 'evt', axis=2, tiled=True)  16.4 us
    ppermute x3, waiting for transfers between devices, product_in_turn(): coming = lax.ppermute(current, axis, right) if hop < count - 1 else None  12 us
    gather x3, local copies, waits for them, and re-layouts, to_depths(): second = jnp.take_along_axis(values, picks + 1, axis=3)  8.62 us
    gather x3, local copies, waits for them, and re-layouts, to_depths(): first = jnp.take_along_axis(values, picks, axis=3)  8.62 us
    dot_general x1, matrix products, body(): rhs_part = jnp.einsum('sek,sec->skc', weighted, data, precision=highest)  7.27 us
    add x1, other arithmetic, body(): jnp.cos(incidence)[:, :, None] * radial  6.81 us
  transfers between devices with their start and end apart: 4, of which 3 were waited for; matrix products, arithmetic and copies ran while one was open for 6% of the time, Pallas kernels for 0%

profile of v1, /device:TPU:0, one launch (start us, length us, event | category | flops | bytes accessed | tf_op | source)
XLA Modules:
  0.0 136.0 jit_solution(9164463858901650917)
XLA Ops:
  6.5 0.8 fusion.25
  7.3 0.7 compare_convert_fusion
  8.0 6.8 %fusion.7 = (f32[8,64,2048]{2,1,0:T(8,128)}, f32[8,64,2048]{2,1,0:T(8,128)}) fusion(bf16[3,8,64,2048]{3,2,1,0:T(8,128)(2,1)} %param.8, f32[8,64]{1,0:T(8,128)S(1)} %get-tuple-element.20, f32[8,64]{1,0:T(8,128)S(1)} %get-tuple-element.15, f32[8,64]{1,0:T(8,128)S(1)} %get-tuple-element.17, f32[8,64]{1,0:T(8,128)S(1)} %get-tuple-element.21), kind=kLoop, calls=%fused_computation.13 | loop fusion | flops 13631488 | bytes 14688256 | tf_op jit(solution)/shard_map/add | solution.py:51
  14.9 7.3 %fusion = f32[8,5,4096]{2,1,0:T(8,128)} fusion(f32[8,64,2048]{2,1,0:T(8,128)} %get-tuple-element.9, f32[8,64,2048]{2,1,0:T(8,128)} %get-tuple-element.8, f32[8,64,5]{1,2,0:T(8,128)S(1)} %stack.19, f32[8,64]{1,0:T(8,128)S(1)} %compare_convert_fusion), kind=kOutput, calls=%fused_computation.2 | convolution fusion | flops 127928832 | bytes 9056256 | tf_op jit(solution)/shard_map/sek,sec->skc/dot_general | solution.py:62
  22.5 30.6 %psum.7 = f32[8,5,5]{1,2,0:T(8,128)S(1)} all-reduce(f32[8,5,5]{1,2,0:T(8,128)S(1)} %fusion.11), channel_id=1, replica_groups=mesh['sta'=4,'evt'=8] {'evt'}, use_global_device_ids=true, to_apply=%region_0.0 | all-reduce | flops 200 | bytes 1600 | tf_op jit(solution)/shard_map/psum | solution.py:63
  53.4 3.7 %custom-call.11 = f32[8,5,5]{2,1,0:T(8,128)S(1)} custom-call(f32[8,5,5]{2,1,0:T(8,128)S(1)} %fusion.18), custom_call_target="Cholesky" | custom-call | tf_op jit(solution)/shard_map/jit(cholesky)/cholesky | solution.py:25
  57.3 3.2 %custom-call.12 = f32[8,1,5,5]{2,3,1,0:T(8,128)S(1)} custom-call(f32[8,1,5,5]{3,2,1,0:T(8,128)S(1)} %select_bitcast_fusion), custom_call_target="InvertDiagBlocksLowerTriangular" | custom-call | tf_op jit(solution)/shard_map/jit(_solve_triangular)/vmap()/triangular_solve | solution.py:27
  61.0 1.2 fusion.16
  62.3 0.3 fusion.14
  62.5 16.4 %all_gather.3 = f32[8,5,4096]{2,1,0:T(8,128)S(1)} all-gather(f32[8,5,512]{2,1,0:T(8,128)S(1)} %fusion.14), channel_id=1, replica_groups=mesh['sta'=4,'evt'=8] {'evt'}, dimensions={2}, use_global_device_ids=true | all-gather | bytes 737280 | tf_op jit(solution)/shard_map/all_gather | solution.py:66
  78.9 0.6 reshape.136
  79.4 17.0 %copy.34 = f32[8,5,2,2048]{1,2,3,0:T(2,128)} copy(f32[8,5,2,2048]{3,2,1,0:T(2,128)S(1)} %reshape.136) | data formatting | bytes 1310720 | tf_op jit(solution)/shard_map/reshape | solution.py:66
  96.4 8.3 %gather_fusion = f32[512,5,2]{1,2,0:T(2,128)S(1)} fusion(f32[8,5,2,2048]{1,2,3,0:T(2,128)} %copy.34, s32[512]{0:T(512)S(1)} %reshape.123), kind=kCustom, calls=%fused_computation.clone | custom fusion | bytes 45056 | tf_op jit(solution)/shard_map/jit(take_along_axis)/gather | solution.py:32
  104.7 0.2 copy.47
  105.0 8.3 %gather_fusion.1 = f32[512,5,2]{1,2,0:T(2,128)S(1)} fusion(f32[8,5,2,2048]{1,2,3,0:T(2,128)} %copy.34, s32[512]{0:T(512)S(1)} %reshape.128), kind=kCustom, calls=%fused_computation.1.clone | custom fusion | bytes 45056 | tf_op jit(solution)/shard_map/jit(take_along_axis)/gather | solution.py:33
  113.3 0.2 copy.49
  113.6 1.5 %collective-permute-start = (f32[8,5,2,64]{3,0,2,1:T(8,128)S(1)}, f32[8,5,2,64]{3,0,2,1:T(8,128)S(1)}, u32[]{:S(2)}, u32[]{:S(2)}) collective-permute-start(f32[8,5,2,64]{3,0,2,1:T(8,128)S(1)} %fusion.13), channel_id=1, source_target_pairs={{0,8},{8,16},{16,24},{24,0},{1,9},{9,17},{17,25},{25,1},{2,10},{10... | collective-permute-start | bytes 61448 | tf_op jit(solution)/shard_map/ppermute | solution.py:17
  115.3 3.2 %collective-permute-done = f32[8,5,2,64]{3,0,2,1:T(8,128)S(1)} collective-permute-done((f32[8,5,2,64]{3,0,2,1:T(8,128)S(1)}, f32[8,5,2,64]{3,0,2,1:T(8,128)S(1)}, u32[]{:S(2)}, u32[]{:S(2)}) %collective-permute-start) | collective-permute-done | bytes 20512 | tf_op jit(solution)/shard_map/ppermute | solution.py:17
  118.5 0.6 collective-permute-start.1
  119.3 4.1 %collective-permute-done.1 = f32[8,5,2,64]{3,0,2,1:T(8,128)S(1)} collective-permute-done((f32[8,5,2,64]{3,0,2,1:T(8,128)S(1)}, f32[8,5,2,64]{3,0,2,1:T(8,128)S(1)}, u32[]{:S(2)}, u32[]{:S(2)}) %collective-permute-start.1) | collective-permute-done | bytes 20512 | tf_op jit(solution)/shard_map/ppermute | solution.py:17
  123.4 0.2 convolution_add_fusion.1
  123.6 4.7 %collective-permute-done.2 = f32[8,5,2,64]{3,0,2,1:T(8,128)S(1)} collective-permute-done((f32[8,5,2,64]{3,0,2,1:T(8,128)S(1)}, f32[8,5,2,64]{3,0,2,1:T(8,128)S(1)}, u32[]{:S(2)}, u32[]{:S(2)}) %collective-permute-start.2) | collective-permute-done | bytes 20512 | tf_op jit(solution)/shard_map/ppermute | solution.py:17
  128.3 0.2 fusion.9
  128.5 0.6 copy.38
  (32 shorter events, 1.7 us)
Async XLA Ops:
  6.5 54.5 %reduce-scatter.2.cloned.1.call-start = ((), (), s32[]{:S(2)}) async-start(), calls=%async_computation.1 | async-start | bytes 1179648 | tf_op jit(solution)/shard_map/reduce_scatter | solution.py:64
  14.9 45.6 %copy-start = (s32[8,512]{1,0:T(8,128)S(1)}, s32[8,512]{1,0:T(8,128)}, u32[]{:S(2)}) copy-start(s32[8,512]{1,0:T(8,128)} %param.12) | copy-start | bytes 49156
  14.9 45.9 %copy-start.1 = (s32[32]{0:T(128)S(1)}, s32[32]{0:T(128)}, u32[]{:S(2)}) copy-start(s32[32]{0:T(128)} %param.13) | copy-start | bytes 388
  113.6 5.0 %collective-permute-start = (f32[8,5,2,64]{3,0,2,1:T(8,128)S(1)}, f32[8,5,2,64]{3,0,2,1:T(8,128)S(1)}, u32[]{:S(2)}, u32[]{:S(2)}) collective-permute-start(f32[8,5,2,64]{3,0,2,1:T(8,128)S(1)} %fusion.13), channel_id=1, source_target_pairs={{0,8},{8,16},{16,24},{24,0},{1,9},{9,17},{17,25},{25,1},{2,10},{10... | collective-permute-start | bytes 61448 | tf_op jit(solution)/shard_map/ppermute | solution.py:17
  118.5 4.9 %collective-permute-start.1 = (f32[8,5,2,64]{3,0,2,1:T(8,128)S(1)}, f32[8,5,2,64]{3,0,2,1:T(8,128)S(1)}, u32[]{:S(2)}, u32[]{:S(2)}) collective-permute-start(f32[8,5,2,64]{3,0,2,1:T(8,128)S(1)} %collective-permute-done), channel_id=1, source_target_pairs={{0,8},{8,16},{16,24},{24,0},{1,9},{9,17},{17,25},{25,1},{2,10},{10... | collective-permute-start | bytes 61448 | tf_op jit(solution)/shard_map/ppermute | solution.py:17
  123.4 4.9 %collective-permute-start.2 = (f32[8,5,2,64]{3,0,2,1:T(8,128)S(1)}, f32[8,5,2,64]{3,0,2,1:T(8,128)S(1)}, u32[]{:S(2)}, u32[]{:S(2)}) collective-permute-start(f32[8,5,2,64]{3,0,2,1:T(8,128)S(1)} %collective-permute-done.1), channel_id=1, source_target_pairs={{0,8},{8,16},{16,24},{24,0},{1,9},{9,17},{17,25},{25,1},{2,10},{10... | collective-permute-start | bytes 61448 | tf_op jit(solution)/shard_map/ppermute | solution.py:17
Sparse Core Ops, SparseCore 0:
  22.3 35.3 reduce-scatter.1
